TPU v7x, 256 devices: a whole 4x4x8 slice. The times are simulated.
256 devices in a mesh: ckpt: 16 (over z, core), rows: 16 (over y, x).
Axes of the slice: x: 4, y: 4, z: 8, core: 2. Of those that a mesh axis runs over, the one named last changes fastest.
Arguments:
- deltas: bfloat16 [16, 4096, 14336], P('ckpt', 'rows'), may hold values from -24 to 24
- start_basis: bfloat16 [16, 14336, 64], P('ckpt', 'rows'), may hold values from -6 to 6
- edit_order: int32 [16], replicated, may hold values from 0 to 15, each once
Outputs:
- merged: bfloat16 [4096, 14336], P('rows', 'ckpt')
Inputs may be any that keep to these rules, and one draw needn't show every extreme that they name: `edit_order`: a permutation: each of 0 to 15 appears once.
All inputs are finite; a program needn't handle non-finite values.
Results may differ from a plain program's by a relative error of at most 0.034.
Values may be sent and summed in bfloat16 or wider, within the bound.
A program may use at most 64 MiB of HBM per device.

v0:
```python
import math
import jax
import jax.numpy as jnp
from jax import lax
from jax.sharding import PartitionSpec as P

RANK = 64
SUB_ITERS = 2
NS_ITERS = 4


def broadcast(value, axis, source):
    kept = jnp.where(lax.axis_index(axis) == source, value, 0).astype(value.dtype)
    return lax.psum(kept, axis)


def solve_right(raw, lower_factor):
    return lax.linalg.triangular_solve(
        lower_factor, raw, left_side=False, lower=True, transpose_a=True
    ).astype(jnp.bfloat16)


def local_gram(raw):
    return jnp.dot(raw.T, raw, precision=lax.Precision.HIGHEST)


def cross_gram(stacked, own_cols):
    return lax.dot_general(
        stacked, own_cols, (((0,), (0,)), ((), ())), preferred_element_type=jnp.float32
    )


def update_cols(own_cols, stacked, gram_cols, lead_factor, tail_factor):
    product = jnp.dot(stacked.astype(jnp.float32), gram_cols, precision=lax.Precision.HIGHEST)
    return (lead_factor * own_cols.astype(jnp.float32) + tail_factor * product).astype(jnp.bfloat16)


def body(deltas, start_basis, edit_order):
    changes = deltas[0]
    basis_now = start_basis[0]
    local_rows = changes.shape[0]
    left_basis = jnp.zeros((local_rows, RANK), jnp.bfloat16)
    lower_factor = jnp.zeros((RANK, RANK), jnp.float32)
    for sweep in range(SUB_ITERS):
        left_raw = jnp.dot(
            changes,
            lax.all_gather(basis_now, "rows", axis=0, tiled=True),
            preferred_element_type=jnp.float32,
        )
        left_gram = lax.psum(local_gram(left_raw), "rows")
        left_basis = solve_right(left_raw, jnp.linalg.cholesky(left_gram))
        right_raw = lax.psum_scatter(
            lax.dot_general(
                changes, left_basis, (((0,), (0,)), ((), ())), preferred_element_type=jnp.float32
            ).astype(jnp.bfloat16),
            "rows",
            scatter_dimension=0,
            tiled=True,
        ).astype(jnp.float32)
        right_gram = lax.psum(local_gram(right_raw), "rows")
        lower_factor = jnp.linalg.cholesky(right_gram)
        basis_now = solve_right(right_raw, lower_factor)
    ckpt_count = lax.axis_size("ckpt")
    rows_count = lax.axis_size("rows")
    ckpt_index = lax.axis_index("ckpt")
    left_now = left_basis
    right_now = basis_now
    for step in range(NS_ITERS):
        left_all, right_all = (
            lax.all_gather(left_now, "ckpt", axis=1, tiled=True),
            lax.all_gather(right_now, "ckpt", axis=1, tiled=True),
        )
        gram_left = cross_gram(left_all, left_now)
        gram_right = cross_gram(right_all, right_now)
        gram_left, gram_right = (
            lax.psum(gram_left.astype(jnp.bfloat16), "rows").astype(jnp.float32),
            lax.psum(gram_right.astype(jnp.bfloat16), "rows").astype(jnp.float32),
        )
        if step == 0:
            lead_factor = 1.5 / math.sqrt(ckpt_count)
            tail_factor = -0.5 / (ckpt_count * math.sqrt(ckpt_count))
        else:
            lead_factor = 1.5
            tail_factor = -0.5
        left_now = update_cols(left_now, left_all, gram_left, lead_factor, tail_factor)
        right_now = update_cols(right_now, right_all, gram_right, lead_factor, tail_factor)
    position = jnp.sum(jnp.where(jnp.arange(ckpt_count) == ckpt_index, edit_order, 0))
    weight_now = (1 + position).astype(jnp.float32) / ckpt_count
    scaled_left = jnp.dot(
        left_now.astype(jnp.float32), lower_factor * weight_now, precision=lax.Precision.HIGHEST
    ).astype(jnp.bfloat16)
    left_stack, right_block = (
        lax.all_gather(scaled_left, "ckpt", axis=1, tiled=True),
        lax.all_gather(right_now, "ckpt", axis=1, tiled=True),
    )
    holder = ckpt_index * rows_count // ckpt_count
    right_held = broadcast(right_block, "rows", holder)
    merged = lax.dot_general(
        left_stack, right_held, (((1,), (1,)), ((), ())), preferred_element_type=jnp.float32
    )
    return merged.astype(jnp.bfloat16)


def solution(mesh):
    return jax.shard_map(
        body,
        mesh=mesh,
        in_specs=(P("ckpt", "rows", None), P("ckpt", "rows", None), P()),
        out_specs=P("rows", "ckpt"),
        check_vma=False,
    )
```

profile of v0, /device:TPU:1, one launch (start us, length us, event | category | flops | bytes accessed | tf_op | source)
XLA Modules:
  0.0 1361.7 jit_solution(2458196330878033833)
XLA Ops:
  6.5 0.7 all-gather.21.cloned.1.call-update
  7.3 54.2 %all-gather.21.cloned.1.call-done = bf16[1,14336,64]{1,2,0:T(8,128)(2,1)} async-done(((bf16[1,896,64]{1,2,0:T(8,128)(2,1)}), bf16[1,14336,64]{1,2,0:T(8,128)(2,1)}) %all-gather.21.cloned.1.call-update) | async-done | bytes 1835024 | tf_op jit(solution)/shard_map/all_gather | solution.py:47
  61.5 5.9 fusion.6
  67.6 58.2 %psum.91 = f32[64,64]{0,1:T(8,128)S(1)} all-reduce(f32[64,64]{0,1:T(8,128)S(1)} %fusion.55), channel_id=1, replica_groups=mesh['ckpt'=16,'rows'=16] {'rows'}, use_global_device_ids=true, to_apply=%region_0.0 | all-reduce | flops 4096 | bytes 32768 | tf_op jit(solution)/shard_map/psum | solution.py:50
  125.9 5.8 cholesky.74
  132.4 0.7 fusion.32
  133.1 4.9 custom-call.10
  138.2 4.5 fusion
  142.7 3.0 copy.24
  145.8 92.6 %reduce-scatter.7.cloned.1.call-done = bf16[896,64]{1,0:T(8,128)(2,1)} async-done(((bf16[14336,64]{1,0:T(8,128)(2,1)}), bf16[896,64]{1,0:T(8,128)(2,1)}) %reduce-scatter.7.cloned.1.call-update) | async-done | bytes 114704
  238.3 1.3 fusion.56
  239.6 57.9 %psum.92 = f32[64,64]{0,1:T(8,128)S(1)} all-reduce(f32[64,64]{0,1:T(8,128)S(1)} %fusion.56), channel_id=1, replica_groups=mesh['ckpt'=16,'rows'=16] {'rows'}, use_global_device_ids=true, to_apply=%region_4.7 | all-reduce | flops 4096 | bytes 32768 | tf_op jit(solution)/shard_map/psum | solution.py:60
  297.6 5.8 cholesky.85
  304.1 0.7 fusion.33
  304.8 4.9 custom-call.11
  309.7 1.1 copy.25
  310.8 1.0 fusion.17
  311.9 60.3 %all-gather.9.cloned.1.call-done = bf16[14336,64]{0,1:T(8,128)(2,1)} async-done(((bf16[896,64]{0,1:T(8,128)(2,1)}), bf16[14336,64]{0,1:T(8,128)(2,1)}) %all-gather.9.cloned.1.call-update) | async-done | bytes 1835024 | tf_op jit(solution)/shard_map/all_gather | solution.py:47
  372.1 6.0 fusion.3
  378.3 58.2 %psum.93 = f32[64,64]{0,1:T(8,128)S(1)} all-reduce(f32[64,64]{0,1:T(8,128)S(1)} %fusion.57), channel_id=1, replica_groups=mesh['ckpt'=16,'rows'=16] {'rows'}, use_global_device_ids=true, to_apply=%region_5.9 | all-reduce | flops 4096 | bytes 32768 | tf_op jit(solution)/shard_map/psum | solution.py:50
  436.6 5.8 cholesky.96
  443.1 0.7 fusion.34
  443.8 4.9 custom-call.12
  449.0 4.5 fusion.1
  453.4 3.0 copy.26
  456.5 92.5 %reduce-scatter.9.cloned.1.call-done = bf16[896,64]{1,0:T(8,128)(2,1)} async-done(((bf16[14336,64]{1,0:T(8,128)(2,1)}), bf16[896,64]{1,0:T(8,128)(2,1)}) %reduce-scatter.9.cloned.1.call-update) | async-done | bytes 114704
  549.0 1.3 fusion.58
  550.3 57.9 %psum.98 = f32[64,64]{0,1:T(8,128)S(1)} all-reduce(f32[64,64]{0,1:T(8,128)S(1)} %fusion.58), channel_id=1, replica_groups=mesh['ckpt'=16,'rows'=16] {'rows'}, use_global_device_ids=true, to_apply=%region_11.15 | all-reduce | flops 4096 | bytes 32768 | tf_op jit(solution)/shard_map/psum | solution.py:60
  608.2 5.8 cholesky.107
  614.1 0.7 compare_reduce_fusion
  615.4 4.9 custom-call.13
  620.3 1.1 copy.27
  621.4 1.0 fusion.18
  622.5 52.0 %all-gather.11.cloned.1.call-done = bf16[896,1024]{0,1:T(8,128)(2,1)} async-done(((bf16[896,64]{0,1:T(8,128)(2,1)}), bf16[896,1024]{0,1:T(8,128)(2,1)}) %all-gather.11.cloned.1.call-update) | async-done | bytes 1835024 | tf_op jit(solution)/shard_map/all_gather | solution.py:71
  674.6 3.0 convolution_convert_fusion.6
  677.6 91.3 %all-reduce.10.cloned.1.call-done = bf16[1024,64]{1,0:T(8,128)(2,1)} async-done(((bf16[1024,64]{1,0:T(8,128)(2,1)}), bf16[1024,64]{1,0:T(8,128)(2,1)}) %all-reduce.10.cloned.1.call-update) | async-done | bytes 131088 | tf_op jit(solution)/shard_map/psum | solution.py:77
  768.9 2.0 fusion.13
  771.0 21.6 %all_gather.38 = bf16[256,1024]{0,1:T(8,128)(2,1)S(1)} all-gather(bf16[256,64]{0,1:T(8,128)(2,1)S(1)} %fusion.24), channel_id=1, replica_groups=mesh['ckpt'=16,'rows'=16] {'ckpt'}, dimensions={1}, use_global_device_ids=true | all-gather | bytes 557056 | tf_op jit(solution)/shard_map/all_gather | solution.py:70
  792.6 1.0 convolution_convert_fusion.10
  793.6 18.5 %all-gather.13.cloned.1.call-done = bf16[896,1024]{0,1:T(8,128)(2,1)} async-done(((bf16[896,64]{0,1:T(8,128)(2,1)}), bf16[896,1024]{0,1:T(8,128)(2,1)}) %all-gather.13.cloned.1.call-update) | async-done | bytes 1835024 | tf_op jit(solution)/shard_map/all_gather | solution.py:71
  812.1 3.0 convolution_convert_fusion.5
  815.1 92.2 %all-reduce.18.cloned.1.call-done = (bf16[1024,64]{1,0:T(8,128)(2,1)}, bf16[1024,64]{1,0:T(8,128)(2,1)}) async-done(((bf16[1024,64]{1,0:T(8,128)(2,1)}, bf16[1024,64]{1,0:T(8,128)(2,1)}), (bf16[1024,64]{1,0:T(8,128)(2,1)}, bf16[1024,64]{1,0:T(8,128)(2,1)})) %all-reduce.18.cloned.1.call-update) | async-done | bytes 262160 | tf_op jit(solution)/shard_map/psum | solution.py:76
  907.4 2.1 fusion.14
  909.8 21.6 %all_gather.39 = bf16[256,1024]{0,1:T(8,128)(2,1)S(1)} all-gather(bf16[256,64]{0,1:T(8,128)(2,1)S(1)} %fusion.25), channel_id=1, replica_groups=mesh['ckpt'=16,'rows'=16] {'ckpt'}, dimensions={1}, use_global_device_ids=true | all-gather | bytes 557056 | tf_op jit(solution)/shard_map/all_gather | solution.py:70
  931.4 1.0 convolution_convert_fusion.9
  932.4 18.3 %all-gather.15.cloned.1.call-done = bf16[896,1024]{0,1:T(8,128)(2,1)} async-done(((bf16[896,64]{0,1:T(8,128)(2,1)}), bf16[896,1024]{0,1:T(8,128)(2,1)}) %all-gather.15.cloned.1.call-update) | async-done | bytes 1835024 | tf_op jit(solution)/shard_map/all_gather | solution.py:71
  950.7 3.0 convolution_convert_fusion.4
  953.8 92.2 %all-reduce.16.cloned.1.call-done = (bf16[1024,64]{1,0:T(8,128)(2,1)}, bf16[1024,64]{1,0:T(8,128)(2,1)}) async-done(((bf16[1024,64]{1,0:T(8,128)(2,1)}, bf16[1024,64]{1,0:T(8,128)(2,1)}), (bf16[1024,64]{1,0:T(8,128)(2,1)}, bf16[1024,64]{1,0:T(8,128)(2,1)})) %all-reduce.16.cloned.1.call-update) | async-done | bytes 262160 | tf_op jit(solution)/shard_map/psum | solution.py:76
  1046.0 2.1 fusion.15
  1048.4 21.6 %all_gather.40 = bf16[256,1024]{0,1:T(8,128)(2,1)S(1)} all-gather(bf16[256,64]{0,1:T(8,128)(2,1)S(1)} %fusion.26), channel_id=1, replica_groups=mesh['ckpt'=16,'rows'=16] {'ckpt'}, dimensions={1}, use_global_device_ids=true | all-gather | bytes 557056 | tf_op jit(solution)/shard_map/all_gather | solution.py:70
  1070.0 1.0 convolution_convert_fusion.8
  1071.0 18.4 %all-gather.17.cloned.1.call-done = bf16[896,1024]{0,1:T(8,128)(2,1)} async-done(((bf16[896,64]{0,1:T(8,128)(2,1)}), bf16[896,1024]{0,1:T(8,128)(2,1)}) %all-gather.17.cloned.1.call-update) | async-done | bytes 1835024 | tf_op jit(solution)/shard_map/all_gather | solution.py:71
  1089.4 3.0 convolution_convert_fusion.3
  1092.4 92.1 %all-reduce.14.cloned.1.call-done = (bf16[1024,64]{1,0:T(8,128)(2,1)}, bf16[1024,64]{1,0:T(8,128)(2,1)}) async-done(((bf16[1024,64]{1,0:T(8,128)(2,1)}, bf16[1024,64]{1,0:T(8,128)(2,1)}), (bf16[1024,64]{1,0:T(8,128)(2,1)}, bf16[1024,64]{1,0:T(8,128)(2,1)})) %all-reduce.14.cloned.1.call-update) | async-done | bytes 262160 | tf_op jit(solution)/shard_map/psum | solution.py:76
  1184.5 2.1 fusion.16
  1187.0 21.6 %all_gather.41 = bf16[256,1024]{0,1:T(8,128)(2,1)S(1)} all-gather(bf16[256,64]{0,1:T(8,128)(2,1)S(1)} %fusion.27), channel_id=1, replica_groups=mesh['ckpt'=16,'rows'=16] {'ckpt'}, dimensions={1}, use_global_device_ids=true | all-gather | bytes 557056 | tf_op jit(solution)/shard_map/all_gather | solution.py:70
  1208.6 1.0 convolution_convert_fusion.7
  1209.6 18.3 %all-gather.19.cloned.1.call-done = bf16[896,1024]{0,1:T(8,128)(2,1)} async-done(((bf16[896,64]{0,1:T(8,128)(2,1)}), bf16[896,1024]{0,1:T(8,128)(2,1)}) %all-gather.19.cloned.1.call-update) | async-done | bytes 1835024 | tf_op jit(solution)/shard_map/all_gather | solution.py:94
  1227.9 1.4 broadcast_select_fusion
  1231.2 98.1 %all-reduce.12.cloned.1.call-done = (bf16[1024,64]{1,0:T(8,128)(2,1)}, bf16[896,1024]{0,1:T(8,128)(2,1)}) async-done(((bf16[1024,64]{1,0:T(8,128)(2,1)}, bf16[896,1024]{0,1:T(8,128)(2,1)}), (bf16[1024,64]{1,0:T(8,128)(2,1)}, bf16[896,1024]{0,1:T(8,128)(2,1)})) %all-reduce.12.cloned.1.call-update) | async-done | bytes 1966096 | tf_op jit(solution)/shard_map/psum | solution.py:76
  1329.3 1.2 fusion.28
  1330.5 0.8 convolution_convert_fusion.11
  1331.3 20.8 %all_gather.42 = bf16[256,1024]{0,1:T(8,128)(2,1)S(1)} all-gather(bf16[256,64]{0,1:T(8,128)(2,1)S(1)} %convolution_convert_fusion.11), channel_id=1, replica_groups=mesh['ckpt'=16,'rows'=16] {'ckpt'}, dimensions={1}, use_global_device_ids=true | all-gather | bytes 557056 | tf_op jit(solution)/shard_map/all_gather | solution.py:93
  1352.1 3.0 convolution_convert_fusion.2
  (75 shorter events, 6.8 us)
Async XLA Ops:
  6.5 54.9 %all-gather.21.cloned.1.call-start = ((), (), s32[]{:S(2)}) async-start(), calls=%async_computation.9 | async-start | bytes 1949696 | tf_op jit(solution)/shard_map/all_gather | solution.py:47
  7.3 231.1 %reduce-scatter.7.cloned.1.call-start = ((), (), s32[]{:S(2)}) async-start(), calls=%async_computation.10 | async-start | bytes 3899392
  145.7 226.4 %all-gather.9.cloned.1.call-start = ((), (), s32[]{:S(2)}) async-start(), calls=%async_computation.2 | async-start | bytes 1949696 | tf_op jit(solution)/shard_map/all_gather | solution.py:47
  311.8 237.2 %reduce-scatter.9.cloned.1.call-start = ((), (), s32[]{:S(2)}) async-start(), calls=%async_computation.11 | async-start | bytes 3899392
  456.4 218.2 %all-gather.11.cloned.1.call-start = ((), (), s32[]{:S(2)}) async-start(), calls=%async_computation.3 | async-start | bytes 1949696 | tf_op jit(solution)/shard_map/all_gather | solution.py:71
  622.5 146.4 %copy-start.7 = (bf16[896,64]{0,1:T(8,128)(2,1)S(1)}, bf16[896,64]{0,1:T(8,128)(2,1)}, u32[]{:S(2)}) copy-start(bf16[896,64]{0,1:T(8,128)(2,1)} %fusion.18) | copy-start | bytes 344068
  622.5 146.4 %all-reduce.10.cloned.1.call-start = ((), (), s32[]{:S(2)}) async-start(), calls=%async_computation.4 | async-start | bytes 524288 | tf_op jit(solution)/shard_map/psum | solution.py:77
  674.6 94.3 %copy-start.3 = (bf16[896,1024]{0,1:T(8,128)(2,1)S(1)}, bf16[896,1024]{0,1:T(8,128)(2,1)}, u32[]{:S(2)}) copy-start(bf16[896,1024]{0,1:T(8,128)(2,1)} %all-gather.11.cloned.1.call-done) | copy-start | bytes 5505028
  677.6 134.5 %all-gather.13.cloned.1.call-start = ((), (), s32[]{:S(2)}) async-start(), calls=%async_computation.5 | async-start | bytes 1949696 | tf_op jit(solution)/shard_map/all_gather | solution.py:71
  771.0 136.4 %all-reduce.18.cloned.1.call-start = ((), (), s32[]{:S(2)}) async-start(), calls=%async_computation.15 | async-start | bytes 1048576 | tf_op jit(solution)/shard_map/psum | solution.py:76
  792.6 114.7 %copy-start.6 = (bf16[896,64]{0,1:T(8,128)(2,1)S(1)}, bf16[896,64]{0,1:T(8,128)(2,1)}, u32[]{:S(2)}) copy-start(bf16[896,64]{0,1:T(8,128)(2,1)} %fusion.13) | copy-start | bytes 344068
  812.1 95.3 %copy-start.2 = (bf16[896,1024]{0,1:T(8,128)(2,1)S(1)}, bf16[896,1024]{0,1:T(8,128)(2,1)}, u32[]{:S(2)}) copy-start(bf16[896,1024]{0,1:T(8,128)(2,1)} %all-gather.13.cloned.1.call-done) | copy-start | bytes 5505028
  815.1 135.7 %all-gather.15.cloned.1.call-start = ((), (), s32[]{:S(2)}) async-start(), calls=%async_computation.6 | async-start | bytes 1949696 | tf_op jit(solution)/shard_map/all_gather | solution.py:71
  907.4 2.2 copy-start.9
  909.4 41.3 %copy-start.4 = (bf16[896,64]{0,1:T(8,128)(2,1)S(1)}, bf16[896,64]{0,1:T(8,128)(2,1)}, u32[]{:S(2)}) copy-start(bf16[896,64]{0,1:T(8,128)(2,1)} %fusion.14) | copy-start | bytes 344068
  909.5 136.5 %all-reduce.16.cloned.1.call-start = ((), (), s32[]{:S(2)}) async-start(), calls=%async_computation.14 | async-start | bytes 1048576 | tf_op jit(solution)/shard_map/psum | solution.py:76
  950.7 95.3 %copy-start = (bf16[896,1024]{0,1:T(8,128)(2,1)S(1)}, bf16[896,1024]{0,1:T(8,128)(2,1)}, u32[]{:S(2)}) copy-start(bf16[896,1024]{0,1:T(8,128)(2,1)} %all-gather.15.cloned.1.call-done) | copy-start | bytes 5505028
  953.7 135.6 %all-gather.17.cloned.1.call-start = ((), (), s32[]{:S(2)}) async-start(), calls=%async_computation.7 | async-start | bytes 1949696 | tf_op jit(solution)/shard_map/all_gather | solution.py:71
  1046.0 2.2 copy-start.10
  1048.1 41.3 %copy-start.5 = (bf16[896,64]{0,1:T(8,128)(2,1)S(1)}, bf16[896,64]{0,1:T(8,128)(2,1)}, u32[]{:S(2)}) copy-start(bf16[896,64]{0,1:T(8,128)(2,1)} %fusion.15) | copy-start | bytes 344068
  1048.1 136.5 %all-reduce.14.cloned.1.call-start = ((), (), s32[]{:S(2)}) async-start(), calls=%async_computation.13 | async-start | bytes 1048576 | tf_op jit(solution)/shard_map/psum | solution.py:76
  1089.3 95.2 %copy-start.1 = (bf16[896,1024]{0,1:T(8,128)(2,1)S(1)}, bf16[896,1024]{0,1:T(8,128)(2,1)}, u32[]{:S(2)}) copy-start(bf16[896,1024]{0,1:T(8,128)(2,1)} %all-gather.17.cloned.1.call-done) | copy-start | bytes 5505028
  1092.3 135.6 %all-gather.19.cloned.1.call-start = ((), (), s32[]{:S(2)}) async-start(), calls=%async_computation.8 | async-start | bytes 1949696 | tf_op jit(solution)/shard_map/all_gather | solution.py:94
  1184.5 2.2 copy-start.8
  1186.6 142.7 %all-reduce.12.cloned.1.call-start = ((), (), s32[]{:S(2)}) async-start(), calls=%async_computation.12 | async-start | bytes 4194304 | tf_op jit(solution)/shard_map/psum | solution.py:76
  1229.3 0.7 copy-start.11
Sparse Core Ops, SparseCore 0:
  9.8 51.6 all-gather.20
  145.8 92.4 reduce-scatter.6
  311.9 60.1 all-gather.8
  456.5 92.4 reduce-scatter.8
  622.6 51.9 all-gather.10
  677.7 91.1 all-reduce.9
  771.1 40.9 all-gather.12
  815.3 92.0 all-reduce.17
  909.6 41.0 all-gather.14
  953.8 92.0 all-reduce.15
  1048.2 41.0 all-gather.16
  1092.5 92.0 all-reduce.13
  1186.8 41.1 all-gather.18
  1231.1 98.1 all-reduce.11
where the time goes:
time: 1360 us
  waiting for transfers between devices  892 us (66%)
  blocking collectives  339 us (25%)
  matrix products  56.3 us (4%)
  other arithmetic  50.3 us (4%)
  between operations  14.1 us (1%)
    psum x4, waiting for transfers between devices, body(): lax.psum(gram_left.astype(jnp.bfloat16), 'rows').astype(jnp.float32)  375 us
    unnamed x16, waiting for transfers between devices  186 us
    all_gather x5, waiting for transfers between devices, body(): lax.all_gather(right_now, 'ckpt', axis=1, tiled=True)  126 us
    psum x2, blocking collectives, body(): left_gram = lax.psum(local_gram(left_raw), 'rows')  116 us
    psum x2, blocking collectives, body(): right_gram = lax.psum(local_gram(right_raw), 'rows')  116 us
    all_gather x2, waiting for transfers between devices, body(): lax.all_gather(basis_now, 'rows', axis=0, tiled=True)  114 us
    psum x1, waiting for transfers between devices, body(): lax.psum(gram_right.astype(jnp.bfloat16), 'rows').astype(jnp.float32)  91.3 us
    all_gather x4, blocking collectives, body(): lax.all_gather(left_now, 'ckpt', axis=1, tiled=True)  86.5 us
  transfers between devices with their start and end apart: 14, of which 14 were waited for; matrix products, arithmetic and copies ran while one was open for 0% of the time, Pallas kernels for 0%

commit v1 on v0

--- a/solution.py
+++ b/solution.py
@@ -47,7 +47,7 @@
             lax.all_gather(basis_now, "rows", axis=0, tiled=True),
             preferred_element_type=jnp.float32,
         )
-        left_gram = lax.psum(local_gram(left_raw), "rows")
+        left_gram = jnp.sum(lax.all_gather(local_gram(left_raw), "rows"), axis=0)
         left_basis = solve_right(left_raw, jnp.linalg.cholesky(left_gram))
         right_raw = lax.psum_scatter(
             lax.dot_general(

time: 1360 us -> 1270 us (0.934)
  blocking collectives: 339 us -> 259 us
    psum x2 -> x0, blocking collectives: 116 us -> none  [body(): left_gram = lax.psum(local_gram(left_raw), 'rows')]
    all_gather x0 -> x2, blocking collectives: none -> 35.8 us  [body(): left_gram = jnp.sum(lax.all_gather(local_gram(left_raw), 'rows'), axis=0)]
where the time goes in v1:
time: 1270 us
  waiting for transfers between devices  879 us (69%)
  blocking collectives  259 us (20%)
  matrix products  56.3 us (4%)
  other arithmetic  50.4 us (4%)
  between operations  14.1 us (1%)
    psum x4, waiting for transfers between devices, body(): lax.psum(gram_left.astype(jnp.bfloat16), 'rows').astype(jnp.float32)  375 us
    unnamed x16, waiting for transfers between devices  174 us
    all_gather x5, waiting for transfers between devices, body(): lax.all_gather(right_now, 'ckpt', axis=1, tiled=True)  126 us
    psum x2, blocking collectives, body(): right_gram = lax.psum(local_gram(right_raw), 'rows')  116 us
    all_gather x2, waiting for transfers between devices, body(): lax.all_gather(basis_now, 'rows', axis=0, tiled=True)  114 us
    psum x1, waiting for transfers between devices, body(): lax.psum(gram_right.astype(jnp.bfloat16), 'rows').astype(jnp.float32)  91.3 us
    all_gather x4, blocking collectives, body(): lax.all_gather(left_now, 'ckpt', axis=1, tiled=True)  86.5 us
    all_gather x2, blocking collectives, body(): left_gram = jnp.sum(lax.all_gather(local_gram(left_raw), 'rows'), axis=0)  35.8 us
  transfers between devices with their start and end apart: 14, of which 14 were waited for; matrix products, arithmetic and copies ran while one was open for 0% of the time, Pallas kernels for 0%

profile of v1, /device:TPU:1, one launch (start us, length us, event | category | flops | bytes accessed | tf_op | source)
XLA Modules:
  0.0 1268.7 jit_solution(13062007667497709708)
XLA Ops:
  6.5 0.7 all-gather.23.cloned.1.call-update
  7.3 54.2 %all-gather.23.cloned.1.call-done = bf16[1,14336,64]{1,2,0:T(8,128)(2,1)} async-done(((bf16[1,896,64]{1,2,0:T(8,128)(2,1)}), bf16[1,14336,64]{1,2,0:T(8,128)(2,1)}) %all-gather.23.cloned.1.call-update) | async-done | bytes 1835024 | tf_op jit(solution)/shard_map/all_gather | solution.py:47
  61.5 5.9 fusion.6
  67.6 17.8 %all-gather.1 = f32[1024,64]{1,0:T(8,128)S(1)} all-gather(f32[64,64]{1,0:T(8,128)S(1)} %fusion.55), channel_id=3, replica_groups=mesh['ckpt'=16,'rows'=16] {'rows'}, dimensions={0}, use_global_device_ids=true | all-gather | bytes 278528 | tf_op jit(solution)/shard_map/all_gather | solution.py:50
  85.6 5.8 cholesky.74
  92.1 0.7 fusion.32
  92.8 4.9 custom-call.10
  97.9 4.5 fusion
  102.4 3.0 copy.18
  105.4 86.3 %reduce-scatter.7.cloned.1.call-done = bf16[896,64]{1,0:T(8,128)(2,1)} async-done(((bf16[14336,64]{1,0:T(8,128)(2,1)}), bf16[896,64]{1,0:T(8,128)(2,1)}) %reduce-scatter.7.cloned.1.call-update) | async-done | bytes 114704
  191.8 1.3 fusion.56
  193.1 57.9 %psum.77 = f32[64,64]{0,1:T(8,128)S(1)} all-reduce(f32[64,64]{0,1:T(8,128)S(1)} %fusion.56), channel_id=1, replica_groups=mesh['ckpt'=16,'rows'=16] {'rows'}, use_global_device_ids=true, to_apply=%region_4.7 | all-reduce | flops 4096 | bytes 32768 | tf_op jit(solution)/shard_map/psum | solution.py:60
  251.0 5.8 cholesky.85
  257.6 0.7 fusion.33
  258.2 4.9 custom-call.11
  263.1 1.1 copy.19
  264.2 1.0 fusion.17
  265.3 60.2 %all-gather.11.cloned.1.call-done = bf16[14336,64]{0,1:T(8,128)(2,1)} async-done(((bf16[896,64]{0,1:T(8,128)(2,1)}), bf16[14336,64]{0,1:T(8,128)(2,1)}) %all-gather.11.cloned.1.call-update) | async-done | bytes 1835024 | tf_op jit(solution)/shard_map/all_gather | solution.py:47
  325.6 6.0 fusion.3
  331.8 18.0 %all-gather.2 = f32[1024,64]{1,0:T(8,128)S(1)} all-gather(f32[64,64]{1,0:T(8,128)S(1)} %fusion.57), channel_id=4, replica_groups=mesh['ckpt'=16,'rows'=16] {'rows'}, dimensions={0}, use_global_device_ids=true | all-gather | bytes 278528 | tf_op jit(solution)/shard_map/all_gather | solution.py:50
  349.9 5.8 cholesky.96
  356.4 0.7 fusion.34
  357.1 4.9 custom-call.12
  362.3 4.5 fusion.1
  366.7 3.0 copy.20
  369.8 86.3 %reduce-scatter.9.cloned.1.call-done = bf16[896,64]{1,0:T(8,128)(2,1)} async-done(((bf16[14336,64]{1,0:T(8,128)(2,1)}), bf16[896,64]{1,0:T(8,128)(2,1)}) %reduce-scatter.9.cloned.1.call-update) | async-done | bytes 114704
  456.1 1.3 fusion.58
  457.3 57.9 %psum.82 = f32[64,64]{0,1:T(8,128)S(1)} all-reduce(f32[64,64]{0,1:T(8,128)S(1)} %fusion.58), channel_id=1, replica_groups=mesh['ckpt'=16,'rows'=16] {'rows'}, use_global_device_ids=true, to_apply=%region_11.15 | all-reduce | flops 4096 | bytes 32768 | tf_op jit(solution)/shard_map/psum | solution.py:60
  515.3 5.8 cholesky.107
  521.2 0.7 compare_reduce_fusion
  522.5 4.9 custom-call.13
  527.4 1.1 copy.21
  528.5 1.0 fusion.18
  529.6 52.0 %all-gather.13.cloned.1.call-done = bf16[896,1024]{0,1:T(8,128)(2,1)} async-done(((bf16[896,64]{0,1:T(8,128)(2,1)}), bf16[896,1024]{0,1:T(8,128)(2,1)}) %all-gather.13.cloned.1.call-update) | async-done | bytes 1835024 | tf_op jit(solution)/shard_map/all_gather | solution.py:71
  581.7 3.0 convolution_convert_fusion.6
  584.7 91.3 %all-reduce.10.cloned.1.call-done = bf16[1024,64]{1,0:T(8,128)(2,1)} async-done(((bf16[1024,64]{1,0:T(8,128)(2,1)}), bf16[1024,64]{1,0:T(8,128)(2,1)}) %all-reduce.10.cloned.1.call-update) | async-done | bytes 131088 | tf_op jit(solution)/shard_map/psum | solution.py:77
  676.0 2.0 fusion.13
  678.1 21.6 %all_gather.54 = bf16[256,1024]{0,1:T(8,128)(2,1)S(1)} all-gather(bf16[256,64]{0,1:T(8,128)(2,1)S(1)} %fusion.24), channel_id=1, replica_groups=mesh['ckpt'=16,'rows'=16] {'ckpt'}, dimensions={1}, use_global_device_ids=true | all-gather | bytes 557056 | tf_op jit(solution)/shard_map/all_gather | solution.py:70
  699.7 1.0 convolution_convert_fusion.10
  700.7 18.5 %all-gather.15.cloned.1.call-done = bf16[896,1024]{0,1:T(8,128)(2,1)} async-done(((bf16[896,64]{0,1:T(8,128)(2,1)}), bf16[896,1024]{0,1:T(8,128)(2,1)}) %all-gather.15.cloned.1.call-update) | async-done | bytes 1835024 | tf_op jit(solution)/shard_map/all_gather | solution.py:71
  719.2 3.0 convolution_convert_fusion.5
  722.2 92.2 %all-reduce.18.cloned.1.call-done = (bf16[1024,64]{1,0:T(8,128)(2,1)}, bf16[1024,64]{1,0:T(8,128)(2,1)}) async-done(((bf16[1024,64]{1,0:T(8,128)(2,1)}, bf16[1024,64]{1,0:T(8,128)(2,1)}), (bf16[1024,64]{1,0:T(8,128)(2,1)}, bf16[1024,64]{1,0:T(8,128)(2,1)})) %all-reduce.18.cloned.1.call-update) | async-done | bytes 262160 | tf_op jit(solution)/shard_map/psum | solution.py:76
  814.5 2.1 fusion.14
  816.9 21.6 %all_gather.55 = bf16[256,1024]{0,1:T(8,128)(2,1)S(1)} all-gather(bf16[256,64]{0,1:T(8,128)(2,1)S(1)} %fusion.25), channel_id=1, replica_groups=mesh['ckpt'=16,'rows'=16] {'ckpt'}, dimensions={1}, use_global_device_ids=true | all-gather | bytes 557056 | tf_op jit(solution)/shard_map/all_gather | solution.py:70
  838.5 1.0 convolution_convert_fusion.9
  839.5 18.3 %all-gather.17.cloned.1.call-done = bf16[896,1024]{0,1:T(8,128)(2,1)} async-done(((bf16[896,64]{0,1:T(8,128)(2,1)}), bf16[896,1024]{0,1:T(8,128)(2,1)}) %all-gather.17.cloned.1.call-update) | async-done | bytes 1835024 | tf_op jit(solution)/shard_map/all_gather | solution.py:71
  857.8 3.0 convolution_convert_fusion.4
  860.9 92.2 %all-reduce.16.cloned.1.call-done = (bf16[1024,64]{1,0:T(8,128)(2,1)}, bf16[1024,64]{1,0:T(8,128)(2,1)}) async-done(((bf16[1024,64]{1,0:T(8,128)(2,1)}, bf16[1024,64]{1,0:T(8,128)(2,1)}), (bf16[1024,64]{1,0:T(8,128)(2,1)}, bf16[1024,64]{1,0:T(8,128)(2,1)})) %all-reduce.16.cloned.1.call-update) | async-done | bytes 262160 | tf_op jit(solution)/shard_map/psum | solution.py:76
  953.0 2.1 fusion.15
  955.5 21.6 %all_gather.56 = bf16[256,1024]{0,1:T(8,128)(2,1)S(1)} all-gather(bf16[256,64]{0,1:T(8,128)(2,1)S(1)} %fusion.26), channel_id=1, replica_groups=mesh['ckpt'=16,'rows'=16] {'ckpt'}, dimensions={1}, use_global_device_ids=true | all-gather | bytes 557056 | tf_op jit(solution)/shard_map/all_gather | solution.py:70
  977.1 1.0 convolution_convert_fusion.8
  978.1 18.3 %all-gather.19.cloned.1.call-done = bf16[896,1024]{0,1:T(8,128)(2,1)} async-done(((bf16[896,64]{0,1:T(8,128)(2,1)}), bf16[896,1024]{0,1:T(8,128)(2,1)}) %all-gather.19.cloned.1.call-update) | async-done | bytes 1835024 | tf_op jit(solution)/shard_map/all_gather | solution.py:71
  996.4 3.0 convolution_convert_fusion.3
  999.4 92.1 %all-reduce.14.cloned.1.call-done = (bf16[1024,64]{1,0:T(8,128)(2,1)}, bf16[1024,64]{1,0:T(8,128)(2,1)}) async-done(((bf16[1024,64]{1,0:T(8,128)(2,1)}, bf16[1024,64]{1,0:T(8,128)(2,1)}), (bf16[1024,64]{1,0:T(8,128)(2,1)}, bf16[1024,64]{1,0:T(8,128)(2,1)})) %all-reduce.14.cloned.1.call-update) | async-done | bytes 262160 | tf_op jit(solution)/shard_map/psum | solution.py:76
  1091.6 2.1 fusion.16
  1094.0 21.6 %all_gather.57 = bf16[256,1024]{0,1:T(8,128)(2,1)S(1)} all-gather(bf16[256,64]{0,1:T(8,128)(2,1)S(1)} %fusion.27), channel_id=1, replica_groups=mesh['ckpt'=16,'rows'=16] {'ckpt'}, dimensions={1}, use_global_device_ids=true | all-gather | bytes 557056 | tf_op jit(solution)/shard_map/all_gather | solution.py:70
  1115.6 1.0 convolution_convert_fusion.7
  1116.6 18.3 %all-gather.21.cloned.1.call-done = bf16[896,1024]{0,1:T(8,128)(2,1)} async-done(((bf16[896,64]{0,1:T(8,128)(2,1)}), bf16[896,1024]{0,1:T(8,128)(2,1)}) %all-gather.21.cloned.1.call-update) | async-done | bytes 1835024 | tf_op jit(solution)/shard_map/all_gather | solution.py:94
  1134.9 1.4 broadcast_select_fusion
  1138.2 98.1 %all-reduce.12.cloned.1.call-done = (bf16[1024,64]{1,0:T(8,128)(2,1)}, bf16[896,1024]{0,1:T(8,128)(2,1)}) async-done(((bf16[1024,64]{1,0:T(8,128)(2,1)}, bf16[896,1024]{0,1:T(8,128)(2,1)}), (bf16[1024,64]{1,0:T(8,128)(2,1)}, bf16[896,1024]{0,1:T(8,128)(2,1)})) %all-reduce.12.cloned.1.call-update) | async-done | bytes 1966096 | tf_op jit(solution)/shard_map/psum | solution.py:76
  1236.3 1.2 fusion.28
  1237.5 0.8 convolution_convert_fusion.11
  1238.4 20.8 %all_gather.58 = bf16[256,1024]{0,1:T(8,128)(2,1)S(1)} all-gather(bf16[256,64]{0,1:T(8,128)(2,1)S(1)} %convolution_convert_fusion.11), channel_id=1, replica_groups=mesh['ckpt'=16,'rows'=16] {'ckpt'}, dimensions={1}, use_global_device_ids=true | all-gather | bytes 557056 | tf_op jit(solution)/shard_map/all_gather | solution.py:93
  1259.2 3.0 convolution_convert_fusion.2
  (77 shorter events, 6.9 us)
Async XLA Ops:
  6.5 54.9 %all-gather.23.cloned.1.call-start = ((), (), s32[]{:S(2)}) async-start(), calls=%async_computation.9 | async-start | bytes 1949696 | tf_op jit(solution)/shard_map/all_gather | solution.py:47
  7.3 184.5 %reduce-scatter.7.cloned.1.call-start = ((), (), s32[]{:S(2)}) async-start(), calls=%async_computation.10 | async-start | bytes 3899392
  105.4 220.2 %all-gather.11.cloned.1.call-start = ((), (), s32[]{:S(2)}) async-start(), calls=%async_computation.2 | async-start | bytes 1949696 | tf_op jit(solution)/shard_map/all_gather | solution.py:47
  265.3 190.8 %reduce-scatter.9.cloned.1.call-start = ((), (), s32[]{:S(2)}) async-start(), calls=%async_computation.11 | async-start | bytes 3899392
  369.7 212.0 %all-gather.13.cloned.1.call-start = ((), (), s32[]{:S(2)}) async-start(), calls=%async_computation.3 | async-start | bytes 1949696 | tf_op jit(solution)/shard_map/all_gather | solution.py:71
  529.6 146.4 %copy-start.7 = (bf16[896,64]{0,1:T(8,128)(2,1)S(1)}, bf16[896,64]{0,1:T(8,128)(2,1)}, u32[]{:S(2)}) copy-start(bf16[896,64]{0,1:T(8,128)(2,1)} %fusion.18) | copy-start | bytes 344068
  529.6 146.4 %all-reduce.10.cloned.1.call-start = ((), (), s32[]{:S(2)}) async-start(), calls=%async_computation.4 | async-start | bytes 524288 | tf_op jit(solution)/shard_map/psum | solution.py:77
  581.7 94.3 %copy-start.3 = (bf16[896,1024]{0,1:T(8,128)(2,1)S(1)}, bf16[896,1024]{0,1:T(8,128)(2,1)}, u32[]{:S(2)}) copy-start(bf16[896,1024]{0,1:T(8,128)(2,1)} %all-gather.13.cloned.1.call-done) | copy-start | bytes 5505028
  584.7 134.5 %all-gather.15.cloned.1.call-start = ((), (), s32[]{:S(2)}) async-start(), calls=%async_computation.5 | async-start | bytes 1949696 | tf_op jit(solution)/shard_map/all_gather | solution.py:71
  678.0 136.4 %all-reduce.18.cloned.1.call-start = ((), (), s32[]{:S(2)}) async-start(), calls=%async_computation.15 | async-start | bytes 1048576 | tf_op jit(solution)/shard_map/psum | solution.py:76
  699.7 114.7 %copy-start.6 = (bf16[896,64]{0,1:T(8,128)(2,1)S(1)}, bf16[896,64]{0,1:T(8,128)(2,1)}, u32[]{:S(2)}) copy-start(bf16[896,64]{0,1:T(8,128)(2,1)} %fusion.13) | copy-start | bytes 344068
  719.2 95.3 %copy-start.2 = (bf16[896,1024]{0,1:T(8,128)(2,1)S(1)}, bf16[896,1024]{0,1:T(8,128)(2,1)}, u32[]{:S(2)}) copy-start(bf16[896,1024]{0,1:T(8,128)(2,1)} %all-gather.15.cloned.1.call-done) | copy-start | bytes 5505028
  722.1 135.7 %all-gather.17.cloned.1.call-start = ((), (), s32[]{:S(2)}) async-start(), calls=%async_computation.6 | async-start | bytes 1949696 | tf_op jit(solution)/shard_map/all_gather | solution.py:71
  814.4 2.2 copy-start.9
  816.5 41.3 %copy-start.4 = (bf16[896,64]{0,1:T(8,128)(2,1)S(1)}, bf16[896,64]{0,1:T(8,128)(2,1)}, u32[]{:S(2)}) copy-start(bf16[896,64]{0,1:T(8,128)(2,1)} %fusion.14) | copy-start | bytes 344068
  816.6 136.5 %all-reduce.16.cloned.1.call-start = ((), (), s32[]{:S(2)}) async-start(), calls=%async_computation.14 | async-start | bytes 1048576 | tf_op jit(solution)/shard_map/psum | solution.py:76
  857.8 95.2 %copy-start = (bf16[896,1024]{0,1:T(8,128)(2,1)S(1)}, bf16[896,1024]{0,1:T(8,128)(2,1)}, u32[]{:S(2)}) copy-start(bf16[896,1024]{0,1:T(8,128)(2,1)} %all-gather.17.cloned.1.call-done) | copy-start | bytes 5505028
  860.8 135.6 %all-gather.19.cloned.1.call-start = ((), (), s32[]{:S(2)}) async-start(), calls=%async_computation.7 | async-start | bytes 1949696 | tf_op jit(solution)/shard_map/all_gather | solution.py:71
  953.0 2.2 copy-start.10
  955.1 41.3 %copy-start.5 = (bf16[896,64]{0,1:T(8,128)(2,1)S(1)}, bf16[896,64]{0,1:T(8,128)(2,1)}, u32[]{:S(2)}) copy-start(bf16[896,64]{0,1:T(8,128)(2,1)} %fusion.15) | copy-start | bytes 344068
  955.1 136.4 %all-reduce.14.cloned.1.call-start = ((), (), s32[]{:S(2)}) async-start(), calls=%async_computation.13 | async-start | bytes 1048576 | tf_op jit(solution)/shard_map/psum | solution.py:76
  996.4 95.1 %copy-start.1 = (bf16[896,1024]{0,1:T(8,128)(2,1)S(1)}, bf16[896,1024]{0,1:T(8,128)(2,1)}, u32[]{:S(2)}) copy-start(bf16[896,1024]{0,1:T(8,128)(2,1)} %all-gather.19.cloned.1.call-done) | copy-start | bytes 5505028
  999.4 135.5 %all-gather.21.cloned.1.call-start = ((), (), s32[]{:S(2)}) async-start(), calls=%async_computation.8 | async-start | bytes 1949696 | tf_op jit(solution)/shard_map/all_gather | solution.py:94
  1091.6 2.2 copy-start.8
  1093.7 142.7 %all-reduce.12.cloned.1.call-start = ((), (), s32[]{:S(2)}) async-start(), calls=%async_computation.12 | async-start | bytes 4194304 | tf_op jit(solution)/shard_map/psum | solution.py:76
  1136.3 0.7 copy-start.11
Sparse Core Ops, SparseCore 0:
  9.8 51.6 all-gather.22
  105.5 86.2 reduce-scatter.6
  265.4 60.1 all-gather.10
  369.8 86.1 reduce-scatter.8
  529.7 51.9 all-gather.12
  584.8 91.1 all-reduce.9
  678.2 40.9 all-gather.14
  722.4 92.0 all-reduce.17
  816.7 41.0 all-gather.16
  860.9 92.0 all-reduce.15
  955.3 41.0 all-gather.18
  999.5 91.9 all-reduce.13
  1093.8 41.1 all-gather.20
  1138.2 98.1 all-reduce.11
